TPU v7x, 256 devices: a whole 4x4x8 slice. The times are simulated.
256 devices in a mesh: row: 16 (over y, x), col: 8 (over z), chan: 2 (over core).
Axes of the slice: x: 4, y: 4, z: 8, core: 2. Of those that a mesh axis runs over, the one named last changes fastest.
Arguments:
- samples: bfloat16 [8192, 2, 8192], P(('chan', 'col'), None, 'row'), parts along dimension 0, may hold values from -6 to 6
- sky_model: bfloat16 [8192, 2, 4096], P(('chan', 'row'), None, 'col'), parts along dimension 0, may hold values from -128 to 128, as said below
- initial_gains: float32 [2, 8192], P(None, ('chan', 'row', 'col')), parts along dimension 1, may hold values from -3 to 3, as said below
Outputs:
- calibrated: float32 [2, 8192], P(None, ('chan', 'row', 'col')), parts along dimension 1
There are 2 independent parts, one for each index of `chan`. A program takes and returns all parts, laid end to end along the dimension named above; each array names one. Nothing has to cross between parts.
Inputs may be any that keep to these rules, and one draw needn't show every extreme that they name: sky_model is Hermitian: sky_model[q,0,p] = sky_model[p,0,q] and sky_model[q,1,p] = -sky_model[p,1,q]. `initial_gains`: every initial gain has magnitude between 0.3 and 3.
All inputs are finite; a program needn't handle non-finite values.
Results may differ from a plain program's by a relative error of at most 0.0003.
Values may be sent and summed in bfloat16 or wider, within the bound.
No kernel may reach another device: no remote copies, remote signals or barrier semaphores. Data moves between devices by JAX's collectives and lax.ppermute only.
A program may use at most 192 MiB of HBM per device.

v0:
```python
import jax
import jax.numpy as jnp
from jax import lax
from jax.sharding import PartitionSpec as P


def vis_tiles(samples):
    block_column = samples.shape[0]
    flattened = samples.reshape(block_column, -1)
    rotated = jnp.concatenate([-samples[:, 1, :], samples[:, 0, :]], axis=1)
    right_side = jnp.concatenate([flattened, rotated], axis=0)
    all_antennas = lax.all_gather(flattened, "col", axis=0, tiled=True)
    vis_tile = lax.psum_scatter(
        lax.dot_general(
            all_antennas, right_side, (((1,), (1,)), ((), ())), preferred_element_type=jnp.float32
        ),
        "row",
        scatter_dimension=0,
        tiled=True,
    )
    return (vis_tile[:, :block_column], vis_tile[:, block_column:])


def exchange(parts, axis):
    count = lax.axis_size(axis)
    copies = jnp.broadcast_to(parts[None], (count,) + parts.shape)
    return lax.all_to_all(copies, axis, 0, 0)


def columns_to_rows(weight_real, weight_imag, power, gain):
    real = gain[0][None, :]
    imag = gain[1][None, :]
    return jnp.stack(
        [
            jnp.sum(weight_real * real + weight_imag * imag, axis=1),
            jnp.sum(weight_real * imag - weight_imag * real, axis=1),
            jnp.sum(power * (real * real + imag * imag), axis=1),
        ]
    )


def rows_to_columns(weight_real, weight_imag, power, gain):
    real = gain[0][:, None]
    imag = gain[1][:, None]
    return jnp.stack(
        [
            jnp.sum(weight_real * real - weight_imag * imag, axis=0),
            jnp.sum(weight_real * imag + weight_imag * real, axis=0),
            jnp.sum(power * (real * real + imag * imag), axis=0),
        ]
    )


def body(samples, sky_model, initial_gains):
    row_count = lax.axis_size("row")
    column_count = lax.axis_size("col")
    row_index = lax.axis_index("row")
    column_index = lax.axis_index("col")
    block_column = samples.shape[0]
    block_row = sky_model.shape[0]
    share_size = initial_gains.shape[1]
    blocks = block_column // block_row
    everything = lax.all_gather(initial_gains, ("row", "col"), axis=1, tiled=True)
    gain = lax.dynamic_slice_in_dim(everything, column_index * block_column, block_column, 1)
    vis_real, vis_imag = vis_tiles(samples)
    model_real = sky_model[:, 0, :].astype(jnp.float32)
    model_imag = sky_model[:, 1, :].astype(jnp.float32)
    global_rows = row_index * block_row + lax.broadcasted_iota(
        jnp.int32, (block_row, block_column), 0
    )
    global_columns = column_index * block_column + lax.broadcasted_iota(
        jnp.int32, (block_row, block_column), 1
    )
    cross_mask = (global_rows != global_columns).astype(jnp.float32)
    weight_real = (vis_real * model_real + vis_imag * model_imag) * cross_mask
    weight_imag = (vis_real * model_imag - vis_imag * model_real) * cross_mask
    power = (model_real * model_real + model_imag * model_imag) * cross_mask
    parts = columns_to_rows(weight_real, weight_imag, power, gain)
    sums = jnp.sum(exchange(parts, "col"), axis=0)
    gain = sums[:2] / sums[2:]
    parts = rows_to_columns(weight_real, weight_imag, power, gain)
    message = jnp.concatenate([parts.reshape(-1), gain.reshape(-1)])
    message = message.reshape(-1, 128)
    received = exchange(message, "row").reshape(row_count, -1)
    sums = jnp.sum(received[:, : 3 * block_column], axis=0).reshape(3, block_column)
    previous = lax.dynamic_slice_in_dim(
        received[:, 3 * block_column :], column_index * blocks, blocks, 0
    )
    previous = previous.reshape(blocks, 2, block_row).transpose(1, 0, 2).reshape(2, block_column)
    gain = 0.5 * (sums[:2] / sums[2:] + previous)
    parts = columns_to_rows(weight_real, weight_imag, power, gain)
    shares = parts.reshape(3, column_count, share_size).transpose(1, 0, 2)
    sums = jnp.sum(lax.all_to_all(shares, "col", 0, 0), axis=0)
    return sums[:2] / sums[2:]


def solution(mesh):
    return jax.shard_map(
        body,
        mesh=mesh,
        in_specs=(
            P(("chan", "col"), None, "row"),
            P(("chan", "row"), None, "col"),
            P(None, ("chan", "row", "col")),
        ),
        out_specs=P(None, ("chan", "row", "col")),
        check_vma=False,
    )
```

profile of v0, /device:TPU:2, one launch (start us, length us, event | category | flops | bytes accessed | tf_op | source)
XLA Modules:
  0.0 509.9 jit_solution(4030947531042781336)
XLA Ops:
  6.5 2.6 copy.35
  9.2 1.5 fusion.11
  10.7 0.1 copy_bitcast_fusion
  10.8 95.5 %all-gather.3.cloned.1.call-done = bf16[4096,1024]{1,0:T(8,128)(2,1)} async-done(((bf16[512,1024]{1,0:T(8,128)(2,1)}), bf16[4096,1024]{1,0:T(8,128)(2,1)}) %all-gather.3.cloned.1.call-update) | async-done | bytes 8388624 | tf_op jit(solution)/shard_map/all_gather | solution.py:12
  106.3 14.5 %convolution_bitcast_fusion = f32[4096,1024]{0,1:T(8,128)} fusion(bf16[4096,1024]{1,0:T(8,128)(2,1)} %all-gather.3.cloned.1.call-done, bf16[512,512]{1,0:T(8,128)(2,1)S(1)} %get-tuple-element.26, bf16[512,512]{1,0:T(8,128)(2,1)S(1)} %get-tuple-element.27, bf16[512,1024]{1,0:T(8,128)(2,1)S(1)} %bitcast.75), kind=kOutput, calls=%fused_computation | convolution fusion | flops 8596226048 | bytes 27262976 | tf_op jit(solution)/shard_map/dot_general | solution.py:14
  120.8 0.6 copy-done.3
  121.5 323.6 %all-gather = f32[128,32,2]{1,2,0:T(2,128)S(1)} all-gather(f32[1,32,2]{1,2,0:T(2,128)S(1)} %bitcast.99), channel_id=1, replica_groups=mesh['row'=16,'col'=8,'chan'=2] {'row','col'}, dimensions={0}, use_global_device_ids=true | all-gather | bytes 33024 | tf_op jit(solution)/shard_map/all_gather | solution.py:63
  445.0 0.1 reshape.71
  445.2 0.7 fusion.12
  445.9 0.5 copy.31
  446.4 0.5 copy.32
  446.9 1.7 add_reduce_fusion.2
  448.6 10.4 %all_to_all.15 = f32[8,3,256]{2,1,0:T(4,128)S(1)} all-to-all(f32[8,3,256]{2,1,0:T(4,128)S(1)} %broadcast_in_dim.6), channel_id=1, replica_groups=mesh['row'=16,'col'=8,'chan'=2] {'col'}, dimensions={0} | all-to-all | bytes 49152 | tf_op jit(solution)/shard_map/all_to_all | solution.py:27
  459.1 0.2 multiply_reduce_fusion.1
  459.4 0.3 subtract_reduce_fusion.1
  459.7 0.6 broadcast_in_dim.15
  460.3 24.4 %all-to-all-start.1 = ((f32[16,16,128]{2,1,0:T(8,128)}), f32[16,16,128]{2,1,0:T(8,128)S(1)}, u32[]{:S(2)}, u32[]{:S(2)}) async-start(f32[16,16,128]{2,1,0:T(8,128)} %broadcast_in_dim.15), calls=%async_computation.2 | async-start | bytes 262144 | tf_op jit(solution)/shard_map/all_to_all | solution.py:27
  484.7 6.7 %all-to-all-done.1 = f32[16,16,128]{2,1,0:T(8,128)S(1)} async-done(((f32[16,16,128]{2,1,0:T(8,128)}), f32[16,16,128]{2,1,0:T(8,128)S(1)}, u32[]{:S(2)}, u32[]{:S(2)}) %all-to-all-start.1) | async-done | bytes 131104 | tf_op jit(solution)/shard_map/all_to_all | solution.py:27
  491.6 0.2 add_reduce_fusion
  491.8 0.1 stack.44
  492.0 0.2 multiply_reduce_fusion
  492.2 0.1 stack.46
  492.3 10.1 %all_to_all.16 = f32[8,3,32]{2,1,0:T(4,128)S(1)} all-to-all(f32[8,3,32]{2,1,0:T(4,128)S(1)} %maximum_bitcast_fusion), channel_id=1, replica_groups=mesh['row'=16,'col'=8,'chan'=2] {'col'}, dimensions={0} | all-to-all | bytes 6144 | tf_op jit(solution)/shard_map/all_to_all | solution.py:93
  502.5 0.6 slice_divide_fusion.1
  (43 shorter events, 0.5 us)
Async XLA Ops:
  6.5 2.6 copy-start
  6.5 99.8 %all-gather.3.cloned.1.call-start = ((), (), s32[]{:S(2)}) async-start(), calls=%async_computation.4 | async-start | bytes 9437184 | tf_op jit(solution)/shard_map/all_gather | solution.py:12
  9.1 97.2 %copy-start.1 = (bf16[64,8,2,512]{3,1,2,0:T(8,128)(2,1)S(1)}, bf16[64,8,2,512]{3,1,2,0:T(8,128)(2,1)}, u32[]{:S(2)}) copy-start(bf16[64,8,2,512]{3,1,2,0:T(8,128)(2,1)} %copy.35) | copy-start | bytes 3145732
  9.1 437.8 %reduce-scatter.2.cloned.1.call-start = ((), (), s32[]{:S(2)}) async-start(), calls=%async_computation.5 | async-start | bytes 17825792 | tf_op jit(solution)/shard_map/reduce_scatter | solution.py:13
  120.8 0.7 copy-start.3
  120.8 324.4 %copy-start.2 = (bf16[256,2,512]{2,1,0:T(2,128)(2,1)S(1)}, bf16[256,2,512]{2,1,0:T(2,128)(2,1)}, u32[]{:S(2)}) copy-start(bf16[256,2,512]{2,1,0:T(2,128)(2,1)} %param.4) | copy-start | bytes 1572868
  460.3 31.1 %all-to-all-start.1 = ((f32[16,16,128]{2,1,0:T(8,128)}), f32[16,16,128]{2,1,0:T(8,128)S(1)}, u32[]{:S(2)}, u32[]{:S(2)}) async-start(f32[16,16,128]{2,1,0:T(8,128)} %broadcast_in_dim.15), calls=%async_computation.2 | async-start | bytes 262144 | tf_op jit(solution)/shard_map/all_to_all | solution.py:27
Sparse Core Ops, SparseCore 0:
  9.2 97.0 all-gather.2
  120.9 114.0 reduce-scatter.1
where the time goes:
time: 510 us
  blocking collectives  344 us (67%)
  waiting for transfers between devices  102 us (20%)
  starting transfers between devices  24.4 us (5%)
  matrix products  14.5 us (3%)
  between operations  13.7 us (3%)
  local copies, waits for them, and re-layouts  7.56 us (1%)
    all_gather x1, blocking collectives, body(): lax.all_gather(initial_gains, ('row', 'col'), axis=1, tiled=True)  324 us
    all_gather x1, waiting for transfers between devices, vis_tiles(): all_antennas = lax.all_gather(flattened, 'col', axis=0, tiled=True)  95.5 us
    all_to_all x1, starting transfers between devices, exchange(): return lax.all_to_all(copies, axis, 0, 0)  24.4 us
    dot_general x1, matrix products, vis_tiles(): lax.dot_general(all_antennas, right_side, (((1,), (1,)), ((), ())), prefe...  14.5 us
    all_to_all x1, blocking collectives, exchange(): return lax.all_to_all(copies, axis, 0, 0)  10.4 us
  transfers between devices with their start and end apart: 3, of which 2 were waited for; matrix products, arithmetic and copies ran while one was open for 1% of the time, Pallas kernels for 0%

commit v1 on v0

--- a/solution.py
+++ b/solution.py
@@ -9,7 +9,9 @@
     flattened = samples.reshape(block_column, -1)
     rotated = jnp.concatenate([-samples[:, 1, :], samples[:, 0, :]], axis=1)
     right_side = jnp.concatenate([flattened, rotated], axis=0)
-    all_antennas = lax.all_gather(flattened, "col", axis=0, tiled=True)
+    all_antennas = jnp.concatenate(
+        lax.all_to_all(jnp.stack([flattened] * lax.axis_size("col")), "col", 0, 0), axis=0
+    )
     vis_tile = lax.psum_scatter(
         lax.dot_general(
             all_antennas, right_side, (((1,), (1,)), ((), ())), preferred_element_type=jnp.float32

time: 510 us -> 607 us (1.19)
  waiting for transfers between devices: 102 us -> 192 us
  starting transfers between devices: 24.4 us -> 33 us
    all_to_all x0 -> x1, waiting for transfers between devices: none -> 185 us  [vis_tiles(): lax.all_to_all(jnp.stack([flattened] * lax.axis_size('col')), 'col', 0, 0)]
    all_gather x1 -> x0, waiting for transfers between devices: 95.5 us -> none  [vis_tiles(): all_antennas = lax.all_gather(flattened, 'col', axis=0, tiled=True)]
    all_to_all x0 -> x1, starting transfers between devices: none -> 8.6 us  [vis_tiles(): lax.all_to_all(jnp.stack([flattened] * lax.axis_size('col')), 'col', 0, 0)]
where the time goes in v1:
time: 607 us; the launch traced here: 606 us
  blocking collectives  339 us (56%)
  waiting for transfers between devices  192 us (32%)
  starting transfers between devices  33 us (5%)
  matrix products  14.5 us (2%)
  between operations  13.7 us (2%)
  local copies, waits for them, and re-layouts  10.8 us (2%)
    all_gather x1, blocking collectives, body(): lax.all_gather(initial_gains, ('row', 'col'), axis=1, tiled=True)  318 us
    all_to_all x1, waiting for transfers between devices, vis_tiles(): lax.all_to_all(jnp.stack([flattened] * lax.axis_size('col')), 'col', 0, 0)  185 us
    all_to_all x1, starting transfers between devices, exchange(): return lax.all_to_all(copies, axis, 0, 0)  24.4 us
    dot_general x1, matrix products, vis_tiles(): lax.dot_general(all_antennas, right_side, (((1,), (1,)), ((), ())), prefe...  14.5 us
  transfers between devices with their start and end apart: 3, of which 2 were waited for; matrix products, arithmetic and copies ran while one was open for 1% of the time, Pallas kernels for 0%

profile of v1, /device:TPU:2, one launch (start us, length us, event | category | flops | bytes accessed | tf_op | source)
XLA Modules:
  0.0 606.2 jit_solution(4252811817936998913)
XLA Ops:
  6.5 1.5 copy.35
  8.0 4.3 stack.39
  12.3 8.6 %all-to-all-start = ((bf16[8,512,1024]{2,1,0:T(8,128)(2,1)}), bf16[8,512,1024]{2,1,0:T(8,128)(2,1)}, u32[]{:S(2)}, u32[]{:S(2)}) async-start(bf16[8,512,1024]{2,1,0:T(8,128)(2,1)} %stack.39), calls=%async_computation | async-start | bytes 16777216 | tf_op jit(solution)/shard_map/all_to_all | solution.py:13
  21.0 1.5 fusion.11
  22.5 0.1 copy_bitcast_fusion
  22.6 184.9 %all-to-all-done = bf16[8,512,1024]{2,1,0:T(8,128)(2,1)} async-done(((bf16[8,512,1024]{2,1,0:T(8,128)(2,1)}), bf16[8,512,1024]{2,1,0:T(8,128)(2,1)}, u32[]{:S(2)}, u32[]{:S(2)}) %all-to-all-start) | async-done | bytes 8388640 | tf_op jit(solution)/shard_map/all_to_all | solution.py:13
  207.5 14.5 %convolution_bitcast_fusion = f32[4096,1024]{0,1:T(8,128)} fusion(bf16[4096,1024]{1,0:T(8,128)(2,1)} %bitcast.2, bf16[512,512]{1,0:T(8,128)(2,1)S(1)} %get-tuple-element.26, bf16[512,512]{1,0:T(8,128)(2,1)S(1)} %get-tuple-element.27, bf16[512,1024]{1,0:T(8,128)(2,1)S(1)} %bitcast.76), kind=kOutput, calls=%fused_computation | convolution fusion | flops 8596226048 | bytes 27262976 | tf_op jit(solution)/shard_map/dot_general | solution.py:16
  222.0 0.6 copy-done.2
  222.7 318.0 %all-gather = f32[128,32,2]{1,2,0:T(2,128)S(1)} all-gather(f32[1,32,2]{1,2,0:T(2,128)S(1)} %bitcast.100), channel_id=1, replica_groups=mesh['row'=16,'col'=8,'chan'=2] {'row','col'}, dimensions={0}, use_global_device_ids=true | all-gather | bytes 33024 | tf_op jit(solution)/shard_map/all_gather | solution.py:65
  540.7 0.1 reshape.77
  540.8 0.7 fusion.12
  541.5 0.5 copy.31
  542.0 0.5 copy.32
  542.6 1.7 add_reduce_fusion.2
  544.3 11.0 %all_to_all.20 = f32[8,3,256]{2,1,0:T(4,128)S(1)} all-to-all(f32[8,3,256]{2,1,0:T(4,128)S(1)} %broadcast_in_dim.6), channel_id=1, replica_groups=mesh['row'=16,'col'=8,'chan'=2] {'col'}, dimensions={0} | all-to-all | bytes 49152 | tf_op jit(solution)/shard_map/all_to_all | solution.py:29
  555.4 0.2 multiply_reduce_fusion.1
  555.7 0.2 subtract_reduce_fusion.1
  556.0 0.6 broadcast_in_dim.15
  556.6 24.4 %all-to-all-start.2 = ((f32[16,16,128]{2,1,0:T(8,128)}), f32[16,16,128]{2,1,0:T(8,128)S(1)}, u32[]{:S(2)}, u32[]{:S(2)}) async-start(f32[16,16,128]{2,1,0:T(8,128)} %broadcast_in_dim.15), calls=%async_computation.3 | async-start | bytes 262144 | tf_op jit(solution)/shard_map/all_to_all | solution.py:29
  581.0 6.7 %all-to-all-done.2 = f32[16,16,128]{2,1,0:T(8,128)S(1)} async-done(((f32[16,16,128]{2,1,0:T(8,128)}), f32[16,16,128]{2,1,0:T(8,128)S(1)}, u32[]{:S(2)}, u32[]{:S(2)}) %all-to-all-start.2) | async-done | bytes 131104 | tf_op jit(solution)/shard_map/all_to_all | solution.py:29
  587.9 0.2 add_reduce_fusion
  588.3 0.2 multiply_reduce_fusion
  588.6 10.1 %all_to_all.21 = f32[8,3,32]{2,1,0:T(4,128)S(1)} all-to-all(f32[8,3,32]{2,1,0:T(4,128)S(1)} %maximum_bitcast_fusion), channel_id=1, replica_groups=mesh['row'=16,'col'=8,'chan'=2] {'col'}, dimensions={0} | all-to-all | bytes 6144 | tf_op jit(solution)/shard_map/all_to_all | solution.py:95
  598.8 0.6 slice_divide_fusion.1
  (41 shorter events, 0.7 us)
Async XLA Ops:
  12.3 8.6 %copy-start = (bf16[512,2,512]{2,1,0:T(2,128)(2,1)S(1)}, bf16[512,2,512]{2,1,0:T(2,128)(2,1)}, u32[]{:S(2)}) copy-start(bf16[512,2,512]{2,1,0:T(2,128)(2,1)} %param.3) | copy-start | bytes 3145732
  12.3 195.2 %all-to-all-start = ((bf16[8,512,1024]{2,1,0:T(8,128)(2,1)}), bf16[8,512,1024]{2,1,0:T(8,128)(2,1)}, u32[]{:S(2)}, u32[]{:S(2)}) async-start(bf16[8,512,1024]{2,1,0:T(8,128)(2,1)} %stack.39), calls=%async_computation | async-start | bytes 16777216 | tf_op jit(solution)/shard_map/all_to_all | solution.py:13
  20.9 521.7 %reduce-scatter.2.cloned.1.call-start = ((), (), s32[]{:S(2)}) async-start(), calls=%async_computation.5 | async-start | bytes 17825792 | tf_op jit(solution)/shard_map/reduce_scatter | solution.py:15
  222.0 0.7 copy-start.2
  222.0 318.8 %copy-start.1 = (bf16[256,2,512]{2,1,0:T(2,128)(2,1)S(1)}, bf16[256,2,512]{2,1,0:T(2,128)(2,1)}, u32[]{:S(2)}) copy-start(bf16[256,2,512]{2,1,0:T(2,128)(2,1)} %param.4) | copy-start | bytes 1572868
  556.6 31.1 %all-to-all-start.2 = ((f32[16,16,128]{2,1,0:T(8,128)}), f32[16,16,128]{2,1,0:T(8,128)S(1)}, u32[]{:S(2)}, u32[]{:S(2)}) async-start(f32[16,16,128]{2,1,0:T(8,128)} %broadcast_in_dim.15), calls=%async_computation.3 | async-start | bytes 262144 | tf_op jit(solution)/shard_map/all_to_all | solution.py:29
Sparse Core Ops, SparseCore 0:
  222.2 111.7 reduce-scatter.1
